TPU v7x, 32 devices: a whole 2x2x4 slice. The times are simulated.
32 devices in a mesh: dp: 8 (over y, x, core), fsdp: 4 (over z).
Axes of the slice: x: 2, y: 2, z: 4, core: 2. Of those that a mesh axis runs over, the one named last changes fastest.
Arguments:
- cells_in: bfloat16 [32, 1024, 768], P(('dp', 'fsdp')), may hold values from -6 to 6
- out_grad: bfloat16 [32, 1024, 768], P(('dp', 'fsdp')), may hold values from -6 to 6
- cell_length: int32 [32], replicated, may hold values from 300 to 1024, as said below
- cell_place: int32 [32], replicated, may hold values from 0 to 31, each once
- gene_ids: int32 [32, 1024], P(('dp', 'fsdp')), may hold values from 0 to 35999
- attn_norm_gain: bfloat16 [768], P('fsdp'), may hold values from 0.5 to 1.5
- attn_norm_bias: bfloat16 [768], P('fsdp'), may hold values from -3 to 3
- query_weight: bfloat16 [768, 768], P('fsdp'), may hold values from -0.21875 to 0.21875
- query_bias: bfloat16 [768], P('fsdp'), may hold values from -3 to 3
- key_weight: bfloat16 [768, 768], P('fsdp'), may hold values from -0.21875 to 0.21875
- value_weight: bfloat16 [768, 768], P('fsdp'), may hold values from -0.21875 to 0.21875
- value_bias: bfloat16 [768], P('fsdp'), may hold values from -3 to 3
- out_weight: bfloat16 [768, 768], P('fsdp'), may hold values from -1.75 to 1.75
- out_bias: bfloat16 [768], P('fsdp'), may hold values from -3 to 3
- ffn_norm_gain: bfloat16 [768], P('fsdp'), may hold values from 0.5 to 1.5
- ffn_norm_bias: bfloat16 [768], P('fsdp'), may hold values from -3 to 3
- up_weight: bfloat16 [768, 3072], P('fsdp'), may hold values from -0.21875 to 0.21875
- up_bias: bfloat16 [3072], P('fsdp'), may hold values from -3 to 3
- down_weight: bfloat16 [3072, 768], P('fsdp'), may hold values from -0.109375 to 0.109375
- down_bias: bfloat16 [768], P('fsdp'), may hold values from -3 to 3
Outputs:
- block_out: bfloat16 [32, 1024, 768], P(('dp', 'fsdp'))
- input_grad: bfloat16 [32, 1024, 768], P(('dp', 'fsdp'))
- grad_attn_norm_gain: float32 [768], P('fsdp')
- grad_attn_norm_bias: float32 [768], P('fsdp')
- grad_query_weight: float32 [768, 768], P('fsdp')
- grad_query_bias: float32 [768], P('fsdp')
- grad_key_weight: float32 [768, 768], P('fsdp')
- grad_value_weight: float32 [768, 768], P('fsdp')
- grad_value_bias: float32 [768], P('fsdp')
- grad_out_weight: float32 [768, 768], P('fsdp')
- grad_out_bias: float32 [768], P('fsdp')
- grad_ffn_norm_gain: float32 [768], P('fsdp')
- grad_ffn_norm_bias: float32 [768], P('fsdp')
- grad_up_weight: float32 [768, 3072], P('fsdp')
- grad_up_bias: float32 [3072], P('fsdp')
- grad_down_weight: float32 [3072, 768], P('fsdp')
- grad_down_bias: float32 [768], P('fsdp')
- gene_counts: int32 [36000], replicated
Inputs may be any that keep to these rules, and one draw needn't show every extreme that they name: `cell_length`: every cell has 300 to 1024 live genes; in every draw one cell has exactly 1024 and another exactly 300. `cell_place`: each cell number appears once.
All inputs are finite; a program needn't handle non-finite values.
Results may differ from a plain program's by a relative error of at most 0.017.
Values may be sent and summed in bfloat16 or wider, within the bound.
No kernel may reach another device: no remote copies, remote signals or barrier semaphores. Data moves between devices by JAX's collectives and lax.ppermute only.
A program may use at most 320 MiB of HBM per device.

v0:
```python
from functools import partial

import jax
import jax.numpy as jnp
from jax import lax
from jax.sharding import PartitionSpec as P

HEADS = 12
HEAD_DIM = 64
VOCAB = 36000


EPSILON = 1e-05
NEGATIVE = -1e30


def normalize(values):
    center = values - jnp.mean(values, axis=-1, keepdims=True)
    inverse = lax.rsqrt(jnp.mean(center * center, axis=-1, keepdims=True) + EPSILON)
    return (center * inverse, inverse)


def norm_back(grad_out, normed, inverse, gain):
    scaled = grad_out * gain
    return inverse * (
        scaled
        - jnp.mean(scaled, axis=-1, keepdims=True)
        - normed * jnp.mean(scaled * normed, axis=-1, keepdims=True)
    )


def project(rows, matrix):
    return jnp.einsum("csd,de->cse", rows, matrix, preferred_element_type=jnp.float32)


def project_back(grads, matrix):
    return jnp.einsum("cse,de->csd", grads, matrix, preferred_element_type=jnp.float32)


def outer_sum(rows, grads):
    return jnp.einsum("csd,cse->de", rows, grads, preferred_element_type=jnp.float32)


def row_total(values):
    return jnp.sum(values.astype(jnp.float32), axis=(0, 1))


def masked_scores(query_block, key_rows, key_live, factor):
    scores = (
        jnp.einsum("cqhe,ckhe->chqk", query_block, key_rows, preferred_element_type=jnp.float32)
        * factor
    )
    return jnp.where(key_live[:, None, None, :], scores, NEGATIVE)


def attend_forward(query_block, key_rows, value_rows, key_live, factor):
    scores = masked_scores(query_block, key_rows, key_live, factor)
    largest = jnp.max(scores, axis=-1, keepdims=True)
    raised = jnp.exp(scores - largest)
    summed = jnp.sum(raised, axis=-1, keepdims=True)
    shares = (raised / summed).astype(jnp.bfloat16)
    blended = jnp.einsum("chqk,ckhe->cqhe", shares, value_rows, preferred_element_type=jnp.float32)
    return (blended, largest + jnp.log(summed))


def attend_backward(query_block, grad_block, key_rows, value_rows, key_live, log_total, factor):
    scores = masked_scores(query_block, key_rows, key_live, factor)
    shares = jnp.exp(scores - log_total)
    grad_values = jnp.einsum(
        "chqk,cqhe->ckhe",
        shares.astype(jnp.bfloat16),
        grad_block,
        preferred_element_type=jnp.float32,
    )
    grad_shares = jnp.einsum(
        "cqhe,ckhe->chqk", grad_block, value_rows, preferred_element_type=jnp.float32
    )
    inner = jnp.sum(shares * grad_shares, axis=-1, keepdims=True)
    grad_scores = (shares * (grad_shares - inner)).astype(jnp.bfloat16)
    grad_queries = factor * jnp.einsum(
        "chqk,ckhe->cqhe", grad_scores, key_rows, preferred_element_type=jnp.float32
    )
    grad_keys = factor * jnp.einsum(
        "chqk,cqhe->ckhe", grad_scores, query_block, preferred_element_type=jnp.float32
    )
    return (grad_queries, grad_keys, grad_values)


def body(
    cells_in,
    out_grad,
    cell_length,
    cell_place,
    gene_ids,
    attn_norm_gain,
    attn_norm_bias,
    query_weight,
    query_bias,
    key_weight,
    value_weight,
    value_bias,
    out_weight,
    out_bias,
    ffn_norm_gain,
    ffn_norm_bias,
    up_weight,
    up_bias,
    down_weight,
    down_bias,
):
    shards = (
        attn_norm_gain,
        attn_norm_bias,
        query_weight,
        query_bias,
        key_weight,
        value_weight,
        value_bias,
        out_weight,
        out_bias,
        ffn_norm_gain,
        ffn_norm_bias,
        up_weight,
        up_bias,
        down_weight,
        down_bias,
    )
    gathered = (
        lax.all_gather(shards[0], "fsdp", axis=0, tiled=True),
        lax.all_gather(shards[1], "fsdp", axis=0, tiled=True),
        lax.all_gather(shards[2], "fsdp", axis=0, tiled=True),
        lax.all_gather(shards[3], "fsdp", axis=0, tiled=True),
        lax.all_gather(shards[4], "fsdp", axis=0, tiled=True),
        lax.all_gather(shards[5], "fsdp", axis=0, tiled=True),
        lax.all_gather(shards[6], "fsdp", axis=0, tiled=True),
        lax.all_gather(shards[7], "fsdp", axis=0, tiled=True),
        lax.all_gather(shards[8], "fsdp", axis=0, tiled=True),
        lax.all_gather(shards[9], "fsdp", axis=0, tiled=True),
        lax.all_gather(shards[10], "fsdp", axis=0, tiled=True),
        lax.all_gather(shards[11], "fsdp", axis=0, tiled=True),
        lax.all_gather(shards[12], "fsdp", axis=0, tiled=True),
        lax.all_gather(shards[13], "fsdp", axis=0, tiled=True),
        lax.all_gather(shards[14], "fsdp", axis=0, tiled=True),
    )
    (
        gain_one,
        shift_one,
        query_w,
        query_b,
        key_w,
        value_w,
        value_b,
        out_w,
        out_b,
        gain_two,
        shift_two,
        up_w,
        up_b,
        down_w,
        down_b,
    ) = gathered
    cell_count = cells_in.shape[0]
    seq_length = cells_in.shape[1]
    model_width = cells_in.shape[2]
    factor = HEAD_DIM ** (-0.5)
    head_shape = (cell_count, seq_length, HEADS, HEAD_DIM)
    slot_index = lax.axis_index(("dp", "fsdp")) * cell_count + jnp.arange(cell_count)
    cell_lens = cell_length[cell_place[slot_index]]
    key_live = jnp.arange(seq_length)[None, :] < cell_lens[:, None]
    block_rows = min(512, seq_length)
    inputs = cells_in.astype(jnp.float32)
    normed_one, inverse_one = normalize(inputs)
    attn_in = (normed_one * gain_one.astype(jnp.float32) + shift_one.astype(jnp.float32)).astype(
        jnp.bfloat16
    )
    query_rows = (
        (project(attn_in, query_w) + query_b.astype(jnp.float32))
        .astype(jnp.bfloat16)
        .reshape(head_shape)
    )
    key_rows = project(attn_in, key_w).astype(jnp.bfloat16).reshape(head_shape)
    value_rows = (
        (project(attn_in, value_w) + value_b.astype(jnp.float32))
        .astype(jnp.bfloat16)
        .reshape(head_shape)
    )
    blended_parts = []
    log_parts = []
    for begin in range(0, seq_length, block_rows):
        query_block = query_rows[:, begin : begin + block_rows]
        blended, log_total = attend_forward(query_block, key_rows, value_rows, key_live, factor)
        blended_parts.append(blended)
        log_parts.append(log_total)
    attn_out = jnp.concatenate(blended_parts, axis=1).reshape(cell_count, seq_length, model_width)
    attn_out = attn_out.astype(jnp.bfloat16)
    residual = inputs + project(attn_out, out_w) + out_b.astype(jnp.float32)
    normed_two, inverse_two = normalize(residual)
    ffn_in = (normed_two * gain_two.astype(jnp.float32) + shift_two.astype(jnp.float32)).astype(
        jnp.bfloat16
    )
    pre_act = project(ffn_in, up_w) + up_b.astype(jnp.float32)
    hidden = jax.nn.gelu(pre_act, approximate=False).astype(jnp.bfloat16)
    result = residual + project(hidden, down_w) + down_b.astype(jnp.float32)
    block_out = result.astype(jnp.bfloat16)
    again = (
        lax.all_gather(shards[0], "fsdp", axis=0, tiled=True),
        lax.all_gather(shards[1], "fsdp", axis=0, tiled=True),
        lax.all_gather(shards[2], "fsdp", axis=0, tiled=True),
        lax.all_gather(shards[3], "fsdp", axis=0, tiled=True),
        lax.all_gather(shards[4], "fsdp", axis=0, tiled=True),
        lax.all_gather(shards[5], "fsdp", axis=0, tiled=True),
        lax.all_gather(shards[6], "fsdp", axis=0, tiled=True),
        lax.all_gather(shards[7], "fsdp", axis=0, tiled=True),
        lax.all_gather(shards[8], "fsdp", axis=0, tiled=True),
        lax.all_gather(shards[9], "fsdp", axis=0, tiled=True),
        lax.all_gather(shards[10], "fsdp", axis=0, tiled=True),
        lax.all_gather(shards[11], "fsdp", axis=0, tiled=True),
        lax.all_gather(shards[12], "fsdp", axis=0, tiled=True),
        lax.all_gather(shards[13], "fsdp", axis=0, tiled=True),
        lax.all_gather(shards[14], "fsdp", axis=0, tiled=True),
    )
    (
        gain_one_b,
        shift_one_b,
        query_wb,
        query_bb,
        key_wb,
        value_wb,
        value_bb,
        out_wb,
        out_bb,
        gain_two_b,
        shift_two_b,
        up_wb,
        up_bb,
        down_wb,
        down_bb,
    ) = again
    grad_down_w = outer_sum(hidden, out_grad)
    grad_down_b = row_total(out_grad)
    grad_hidden = project_back(out_grad, down_wb)
    unused_value, gelu_back = jax.vjp(partial(jax.nn.gelu, approximate=False), pre_act)
    grad_pre = gelu_back(grad_hidden)[0].astype(jnp.bfloat16)
    grad_up_w = outer_sum(ffn_in, grad_pre)
    grad_up_b = row_total(grad_pre)
    grad_ffn_in = project_back(grad_pre, up_wb)
    grad_gain_two = jnp.sum(grad_ffn_in * normed_two, axis=(0, 1))
    grad_shift_two = jnp.sum(grad_ffn_in, axis=(0, 1))
    grad_residual = out_grad.astype(jnp.float32) + norm_back(
        grad_ffn_in, normed_two, inverse_two, gain_two_b.astype(jnp.float32)
    )
    grad_branch = grad_residual.astype(jnp.bfloat16)
    grad_out_w = outer_sum(attn_out, grad_branch)
    grad_out_b = row_total(grad_branch)
    grad_mixed = project_back(grad_branch, out_wb).astype(jnp.bfloat16).reshape(head_shape)
    grad_keys = jnp.zeros(head_shape, jnp.float32)
    grad_values = jnp.zeros(head_shape, jnp.float32)
    query_parts = []
    for number, begin in enumerate(range(0, seq_length, block_rows)):
        query_block = query_rows[:, begin : begin + block_rows]
        grad_block = grad_mixed[:, begin : begin + block_rows]
        part_queries, part_keys, part_values = attend_backward(
            query_block, grad_block, key_rows, value_rows, key_live, log_parts[number], factor
        )
        query_parts.append(part_queries)
        grad_keys = grad_keys + part_keys
        grad_values = grad_values + part_values
    flat_shape = (cell_count, seq_length, model_width)
    grad_query_rows = jnp.concatenate(query_parts, axis=1).reshape(flat_shape).astype(jnp.bfloat16)
    grad_key_rows = grad_keys.reshape(flat_shape).astype(jnp.bfloat16)
    grad_value_rows = grad_values.reshape(flat_shape).astype(jnp.bfloat16)
    grad_query_w = outer_sum(attn_in, grad_query_rows)
    grad_query_b = row_total(grad_query_rows)
    grad_key_w = outer_sum(attn_in, grad_key_rows)
    grad_value_w = outer_sum(attn_in, grad_value_rows)
    grad_value_b = row_total(grad_value_rows)
    grad_attn_in = (
        project_back(grad_query_rows, query_wb)
        + project_back(grad_key_rows, key_wb)
        + project_back(grad_value_rows, value_wb)
    )
    grad_gain_one = jnp.sum(grad_attn_in * normed_one, axis=(0, 1))
    grad_shift_one = jnp.sum(grad_attn_in, axis=(0, 1))
    input_grad = (
        grad_residual
        + norm_back(grad_attn_in, normed_one, inverse_one, gain_one_b.astype(jnp.float32))
    ).astype(jnp.bfloat16)
    local_grads = (
        grad_gain_one,
        grad_shift_one,
        grad_query_w,
        grad_query_b,
        grad_key_w,
        grad_value_w,
        grad_value_b,
        grad_out_w,
        grad_out_b,
        grad_gain_two,
        grad_shift_two,
        grad_up_w,
        grad_up_b,
        grad_down_w,
        grad_down_b,
    )
    shard_grads = (
        lax.psum_scatter(
            local_grads[0].astype(jnp.bfloat16), "fsdp", scatter_dimension=0, tiled=True
        ).astype(jnp.float32),
        lax.psum_scatter(
            local_grads[1].astype(jnp.bfloat16), "fsdp", scatter_dimension=0, tiled=True
        ).astype(jnp.float32),
        lax.psum_scatter(
            local_grads[2].astype(jnp.bfloat16), "fsdp", scatter_dimension=0, tiled=True
        ).astype(jnp.float32),
        lax.psum_scatter(
            local_grads[3].astype(jnp.bfloat16), "fsdp", scatter_dimension=0, tiled=True
        ).astype(jnp.float32),
        lax.psum_scatter(
            local_grads[4].astype(jnp.bfloat16), "fsdp", scatter_dimension=0, tiled=True
        ).astype(jnp.float32),
        lax.psum_scatter(
            local_grads[5].astype(jnp.bfloat16), "fsdp", scatter_dimension=0, tiled=True
        ).astype(jnp.float32),
        lax.psum_scatter(
            local_grads[6].astype(jnp.bfloat16), "fsdp", scatter_dimension=0, tiled=True
        ).astype(jnp.float32),
        lax.psum_scatter(
            local_grads[7].astype(jnp.bfloat16), "fsdp", scatter_dimension=0, tiled=True
        ).astype(jnp.float32),
        lax.psum_scatter(
            local_grads[8].astype(jnp.bfloat16), "fsdp", scatter_dimension=0, tiled=True
        ).astype(jnp.float32),
        lax.psum_scatter(
            local_grads[9].astype(jnp.bfloat16), "fsdp", scatter_dimension=0, tiled=True
        ).astype(jnp.float32),
        lax.psum_scatter(
            local_grads[10].astype(jnp.bfloat16), "fsdp", scatter_dimension=0, tiled=True
        ).astype(jnp.float32),
        lax.psum_scatter(
            local_grads[11].astype(jnp.bfloat16), "fsdp", scatter_dimension=0, tiled=True
        ).astype(jnp.float32),
        lax.psum_scatter(
            local_grads[12].astype(jnp.bfloat16), "fsdp", scatter_dimension=0, tiled=True
        ).astype(jnp.float32),
        lax.psum_scatter(
            local_grads[13].astype(jnp.bfloat16), "fsdp", scatter_dimension=0, tiled=True
        ).astype(jnp.float32),
        lax.psum_scatter(
            local_grads[14].astype(jnp.bfloat16), "fsdp", scatter_dimension=0, tiled=True
        ).astype(jnp.float32),
    )
    total_grads = lax.psum(
        (
            shard_grads[0],
            shard_grads[1],
            shard_grads[2],
            shard_grads[3],
            shard_grads[4],
            shard_grads[5],
            shard_grads[6],
            shard_grads[7],
            shard_grads[8],
            shard_grads[9],
            shard_grads[10],
            shard_grads[11],
            shard_grads[12],
            shard_grads[13],
            shard_grads[14],
        ),
        "dp",
    )
    live_rows = key_live.astype(jnp.int32).reshape(-1)
    local_tally = jax.ops.segment_sum(live_rows, gene_ids.reshape(-1), num_segments=VOCAB)
    gene_counts = lax.psum(local_tally, ("dp", "fsdp"))
    return (block_out, input_grad) + tuple(total_grads) + (gene_counts,)


def solution(mesh):
    in_specs = (
        P(("dp", "fsdp"), None, None),
        P(("dp", "fsdp"), None, None),
        P(),
        P(),
        P(("dp", "fsdp"), None),
        P("fsdp"),
        P("fsdp"),
        P("fsdp", None),
        P("fsdp"),
        P("fsdp", None),
        P("fsdp", None),
        P("fsdp"),
        P("fsdp", None),
        P("fsdp"),
        P("fsdp"),
        P("fsdp"),
        P("fsdp", None),
        P("fsdp"),
        P("fsdp", None),
        P("fsdp"),
    )
    out_specs = (
        P(("dp", "fsdp"), None, None),
        P(("dp", "fsdp"), None, None),
        P("fsdp"),
        P("fsdp"),
        P("fsdp", None),
        P("fsdp"),
        P("fsdp", None),
        P("fsdp", None),
        P("fsdp"),
        P("fsdp", None),
        P("fsdp"),
        P("fsdp"),
        P("fsdp"),
        P("fsdp", None),
        P("fsdp"),
        P("fsdp", None),
        P("fsdp"),
        P(),
    )
    return jax.shard_map(body, mesh=mesh, in_specs=in_specs, out_specs=out_specs, check_vma=False)
```

profile of v0, /device:TPU:0, one launch (start us, length us, event | category | flops | bytes accessed | tf_op | source)
XLA Modules:
  0.0 887.1 jit_solution(17964018789656444972)
XLA Ops:
  17.0 21.2 %all-reduce.19 = (bf16[768]{0:T(1024)(128)(2,1)S(1)}, bf16[768]{0:T(1024)(128)(2,1)S(1)}, bf16[768]{0:T(1024)(128)(2,1)S(1)}, bf16[768]{0:T(1024)(128)(2,1)S(1)}...) all-reduce(bf16[768]{0:T(1024)(128)(2,1)S(1)} %dynamic-update-slice, ...), channel_id=1, replica_groups=mesh['dp'=8,'fsdp'=4] {'fsdp'}, use_global_device_ids=true, to_apply=%add.1 | all-reduce | flops 5376 | bytes 21504
  42.8 13.3 %all-gather = bf16[4,1,768]{2,1,0:T(2,128)(2,1)S(1)} all-gather(bf16[1,1,768]{2,1,0:T(2,128)(2,1)S(1)} %reshape.630), channel_id=1, replica_groups=mesh['dp'=8,'fsdp'=4] {'fsdp'}, dimensions={0}, use_global_device_ids=true | all-gather | bytes 7680 | tf_op jit(solution)/shard_map/all_gather | solution.py:141
  60.6 14.8 %all-gather.10.cloned.1.call-done = bf16[768,768]{1,0:T(8,128)(2,1)} async-done(((bf16[192,768]{1,0:T(8,128)(2,1)}), bf16[768,768]{1,0:T(8,128)(2,1)}) %all-gather.10.cloned.1.call-update) | async-done | bytes 1179664 | tf_op jit(solution)/shard_map/all_gather | solution.py:131
  78.3 10.4 %fusion.18 = (f32[12,512]{1,0:T(8,128)S(1)}, f32[12,512,1024]{2,1,0:T(8,128)}) fusion(pred[1024]{0:T(1024)(128)(4,1)S(1)} %iota_compare_fusion, bf16[1024,12,64]{0,2,1:T(8,128)(2,1)S(1)} %bitcast.160, bf16[1,1024,12,64]{1,3,2,0:T(8,128)(2,1)S(1)} %bitcast.168), kind=kOutput, calls=%fused_computation.40 | convolution fusion | flops 824174592 | bytes 27550720 | tf_op jit(solution)/shard_map/cqhe,ckhe->chqk/dot_general | solution.py:50
  88.7 20.6 %fusion = (f32[12,512]{1,0:T(8,128)S(1)}, f32[12,512]{1,0:T(8,128)S(1)}, f32[12,512,1024]{2,1,0:T(8,128)}) fusion(f32[12,512]{1,0:T(8,128)S(1)} %get-tuple-element.128, f32[12,512,1024]{2,1,0:T(8,128)} %get-tuple-element.129, pred[1024]{0:T(1024)(128)(4,1)S(1)} %iota_compare_fusion, bf16[1024,12,64]{0,2,1:T(8,128)(2,1)S(1)} %bitcast.161, ...), kind=kOutput, calls=%fused_computation.13 | convolution fusion | flops 849334272 | bytes 52765696 | tf_op jit(solution)/shard_map/cqhe,ckhe->chqk/dot_general | solution.py:50
  112.2 12.0 %fusion.67 = bf16[12,64,512]{2,1,0:T(8,128)(2,1)S(1)} fusion(bf16[1024,12,64]{0,2,1:T(8,128)(2,1)S(1)} %bitcast.164, f32[12,512]{1,0:T(8,128)S(1)} %get-tuple-element.84, f32[12,512]{1,0:T(8,128)S(1)} %get-tuple-element.128, f32[12,512,1024]{2,1,0:T(8,128)} %get-tuple-element.129, pred[1024]{0:T(1024)(128)(4,1)S(1)} %iota_compare_fusion), kind=kOutput, calls=%fused_computation.109 | convolution fusion | flops 837156864 | bytes 27575296 | tf_op jit(solution)/shard_map/chqk,ckhe->cqhe/dot_general | solution.py:62
  124.3 11.5 %fusion.1 = f32[12,512]{1,0:T(8,128)S(1)} fusion(f32[12,512]{1,0:T(8,128)S(1)} %get-tuple-element.85, f32[12,512,1024]{2,1,0:T(8,128)} %get-tuple-element.130, pred[1024]{0:T(1024)(128)(4,1)S(1)} %iota_compare_fusion), kind=kLoop, calls=%fused_computation.14 | loop fusion | flops 25159680 | bytes 25216000 | tf_op jit(solution)/shard_map/reduce_sum | solution.py:60
  135.8 11.2 %fusion.66 = bf16[12,64,512]{2,1,0:T(8,128)(2,1)S(1)} fusion(bf16[1024,12,64]{0,2,1:T(8,128)(2,1)S(1)} %bitcast.165, f32[12,512]{1,0:T(8,128)S(1)} %fusion.1, f32[12,512]{1,0:T(8,128)S(1)} %get-tuple-element.85, f32[12,512,1024]{2,1,0:T(8,128)} %get-tuple-element.130, pred[1024]{0:T(1024)(128)(4,1)S(1)} %iota_compare_fusion), kind=kOutput, calls=%fused_computation.108 | convolution fusion | flops 837156864 | bytes 27575296 | tf_op jit(solution)/shard_map/chqk,ckhe->cqhe/dot_general | solution.py:62
  153.2 74.3 %all-gather.16.cloned.1.call-done = bf16[768,3072]{1,0:T(8,128)(2,1)} async-done(((bf16[192,3072]{1,0:T(8,128)(2,1)}), bf16[768,3072]{1,0:T(8,128)(2,1)}) %all-gather.16.cloned.1.call-update) | async-done | bytes 4718608 | tf_op jit(solution)/shard_map/all_gather | solution.py:140
  227.6 38.2 %multiply_convert_fusion.2 = (bf16[1024,3072]{1,0:T(8,128)(2,1)}, f32[1024,3072]{1,0:T(8,128)}, f32[1024,3072]{1,0:T(8,128)}) fusion(f32[3072]{0:T(1024)S(1)} %bitcast.188, bf16[768,3072]{1,0:T(8,128)(2,1)} %all-gather.16.cloned.1.call-done, f32[1,1024,768]{1,2,0:T(8,128)} %copy-done.3, f32[768]{0:T(1024)S(1)} %convert_element_type.273, ...), kind=kOutput, calls=%fused_computation.24 | convolution fusion | flops 5043388416 | bytes 39348224 | tf_op jit(solution)/shard_map/csd,de->cse/dot_general | solution.py:33
  265.7 51.2 %all-gather.18.cloned.1.call-done = bf16[3072,768]{1,0:T(8,128)(2,1)} async-done(((bf16[768,768]{1,0:T(8,128)(2,1)}), bf16[3072,768]{1,0:T(8,128)(2,1)}) %all-gather.18.cloned.1.call-update) | async-done | bytes 4718608 | tf_op jit(solution)/shard_map/all_gather | solution.py:142
  317.0 17.3 %fusion.104 = (bf16[3072]{0:T(1024)(128)(2,1)}, bf16[1024,3072]{1,0:T(8,128)(2,1)}) fusion(f32[1024,3072]{1,0:T(8,128)} %get-tuple-element.123, bf16[3072,768]{1,0:T(8,128)(2,1)} %all-gather.18.cloned.1.call-done, bf16[1,1024,768]{2,1,0:T(8,128)(2,1)S(1)} %copy-done.12, f32[1024,3072]{1,0:T(8,128)} %get-tuple-element.133, f32[3072]{0:T(1024)S(1)} %bitcast.189), kind=kOutput, calls=%fused_computation.161 | convolution fusion | flops 4882166784 | bytes 37767168 | tf_op jit(solution)/shard_map/cse,de->csd/dot_general | solution.py:37
  334.3 10.5 %fusion.103 = (bf16[768]{0:T(1024)(128)(2,1)}, f32[1024,768]{1,0:T(8,128)}) fusion(bf16[1024,3072]{1,0:T(8,128)(2,1)} %get-tuple-element.141, bf16[768,3072]{1,0:T(8,128)(2,1)} %all-gather.16.cloned.1.call-done), kind=kOutput, calls=%fused_computation.160 | convolution fusion | flops 4832623616 | bytes 14157312 | tf_op jit(solution)/shard_map/cse,de->csd/dot_general | solution.py:37
  360.6 10.4 %fusion.72 = f32[12,512,1024]{2,1,0:T(8,128)} fusion(bf16[1024,12,64]{0,2,1:T(8,128)(2,1)S(1)} %bitcast.166, bf16[1,1024,12,64]{1,3,2,0:T(8,128)(2,1)S(1)} %bitcast.174), kind=kOutput, calls=%fused_computation.118 | convolution fusion | flops 805306368 | bytes 27525120 | tf_op jit(solution)/shard_map/cqhe,ckhe->chqk/dot_general | solution.py:75
  371.0 35.5 %multiply_reduce_fusion.1 = (f32[12,512]{1,0:T(8,128)S(1)}, f32[12,512]{1,0:T(8,128)S(1)}, f32[12,512,1024]{2,1,0:T(8,128)}) fusion(f32[12,512]{1,0:T(8,128)S(1)} %copy-done.28, f32[12,512,1024]{2,1,0:T(8,128)} %get-tuple-element.129, pred[1024]{0:T(1024)(128)(4,1)S(1)} %copy-done.37, f32[12,512,1024]{2,1,0:T(8,128)} %fusion.72, ...), kind=kOutput, calls=%fused_computation.5 | convolution fusion | flops 868208640 | bytes 103138304 | tf_op jit(solution)/shard_map/cqhe,ckhe->chqk/dot_general | solution.py:75
  406.5 41.7 %multiply_convert_fusion.1 = (bf16[12,512,1024]{2,1,0:T(8,128)(2,1)}, bf16[12,512,1024]{2,1,0:T(8,128)(2,1)}) fusion(f32[12,512,1024]{2,1,0:T(8,128)} %get-tuple-element.134, f32[12,512]{1,0:T(8,128)S(1)} %get-tuple-element.82, f32[12,512]{1,0:T(8,128)S(1)} %copy-done.28, f32[12,512,1024]{2,1,0:T(8,128)} %get-tuple-element.129, ...), kind=kLoop, calls=%fused_computation.4 | loop fusion | flops 75497472 | bytes 125928448 | tf_op jit(solution)/shard_map/convert_element_type | solution.py:79
  448.1 10.1 %multiply_bitcast_fusion.1 = bf16[1,512,12,64]{1,3,2,0:T(8,128)(2,1)} fusion(bf16[1024,12,64]{0,2,1:T(8,128)(2,1)} %bitcast.162, bf16[12,512,1024]{2,1,0:T(8,128)(2,1)} %get-tuple-element.124), kind=kOutput, calls=%fused_computation.103 | convolution fusion | flops 806092800 | bytes 14942208 | tf_op jit(solution)/shard_map/chqk,ckhe->cqhe/dot_general | solution.py:80
  487.8 10.7 %fusion.5 = f32[12,64,1024]{2,1,0:T(8,128)S(1)} fusion(f32[12,512]{1,0:T(8,128)S(1)} %copy-done.29, f32[12,512,1024]{2,1,0:T(8,128)} %get-tuple-element.130, pred[1024]{0:T(1024)(128)(4,1)S(1)} %copy-done.37, bf16[1,1024,12,64]{1,3,2,0:T(8,128)(2,1)S(1)} %bitcast.176), kind=kOutput, calls=%fused_computation.19 | convolution fusion | flops 830472192 | bytes 29131776 | tf_op jit(solution)/shard_map/chqk,cqhe->ckhe/dot_general | solution.py:69
  498.5 11.5 %bitcast_reduce_fusion = (bf16[12,64]{1,0:T(8,128)(2,1)S(1)}, bf16[12,64,1024]{2,1,0:T(8,128)(2,1)S(1)}) fusion(f32[12,64,1024]{2,1,0:T(8,128)S(1)} %fusion.5, f32[12,512]{1,0:T(8,128)S(1)} %copy-done.28, f32[12,512,1024]{2,1,0:T(8,128)} %get-tuple-element.129, pred[1024]{0:T(1024)(128)(4,1)S(1)} %copy-done.37, bf16[1,1024,12,64]{1,3,2,0:T(8,128)(2,1)S(1)} %bitcast.177), kind=kOutput, calls=%fused_computation.97 | convolution fusion | flops 832830720 | bytes 30706176 | tf_op jit(solution)/shard_map/chqk,cqhe->ckhe/dot_general | solution.py:69
  514.0 9.9 %convolution_convert_fusion.1 = bf16[768,3072]{1,0:T(8,128)(2,1)} fusion(bf16[1024,3072]{1,0:T(8,128)(2,1)} %get-tuple-element.141, f32[1,1024,768]{1,2,0:T(8,128)} %copy-done.3, f32[768]{0:T(1024)S(1)} %copy-done.44, f32[768]{0:T(1024)S(1)} %convert_element_type.272, f32[1024]{0:T(1024)S(1)} %add_rsqrt_fusion, f32[1024]{0:T(1024)S(1)} %broadcast_multiply_fusion.4), kind=kOutput, calls=%fused_computation.43 | convolution fusion | flops 4838129664 | bytes 14170112 | tf_op jit(solution)/shard_map/csd,cse->de/dot_general | solution.py:41
  553.8 16.2 %all-reduce.18 = (bf16[768]{0:T(1024)(128)(2,1)S(1)}, bf16[768]{0:T(1024)(128)(2,1)S(1)}, bf16[768]{0:T(1024)(128)(2,1)S(1)}, bf16[768]{0:T(1024)(128)(2,1)S(1)}...) all-reduce(bf16[768]{0:T(1024)(128)(2,1)S(1)} %dynamic-update-slice, ...), channel_id=1, replica_groups=mesh['dp'=8,'fsdp'=4] {'fsdp'}, use_global_device_ids=true, to_apply=%add.7 | all-reduce | flops 9984 | bytes 39936
  590.5 53.6 %reduce-scatter.15.cloned.1.call-done = bf16[192,3072]{1,0:T(8,128)(2,1)} async-done(((bf16[768,3072]{1,0:T(8,128)(2,1)}), bf16[192,3072]{1,0:T(8,128)(2,1)}) %reduce-scatter.15.cloned.1.call-update) | async-done | bytes 1179664 | tf_op jit(solution)/shard_map/reduce_scatter | solution.py:339
  644.2 88.4 %reduce-scatter.17.cloned.1.call-done = bf16[768,768]{1,0:T(8,128)(2,1)} async-done(((bf16[3072,768]{1,0:T(8,128)(2,1)}), bf16[768,768]{1,0:T(8,128)(2,1)}) %reduce-scatter.17.cloned.1.call-update) | async-done | bytes 1179664 | tf_op jit(solution)/shard_map/reduce_scatter | solution.py:345
  732.5 145.3 %all-reduce.24 = (f32[192]{0:T(256)}, f32[192]{0:T(256)}, f32[192,768]{1,0:T(8,128)}, f32[192]{0:T(256)}, f32[192,768]{1,0:T(8,128)}, /*index=5*/f32[192,768]{1,...) all-reduce(f32[192]{0:T(256)S(1)} %dynamic-slice_convert_fusion.8, ...), channel_id=1, replica_groups=mesh['dp'=8,'fsdp'=4] {'dp'}, use_global_device_ids=true, to_apply=%region_16.17 | all-reduce | flops 1771776 | bytes 10635264 | tf_op jit(solution)/shard_map/psum | solution.py:352
  (240 shorter events, 126.7 us)
Async XLA Ops:
  8.1 49.6 %all-gather.12.cloned.1.call-start = ((), (), s32[]{:S(2)}) async-start(), calls=%async_computation.8 | async-start | bytes 1474560 | tf_op jit(solution)/shard_map/all_gather | solution.py:133
  8.9 66.5 %all-gather.10.cloned.1.call-start = ((), (), s32[]{:S(2)}) async-start(), calls=%async_computation.7 | async-start | bytes 1474560 | tf_op jit(solution)/shard_map/all_gather | solution.py:131
  9.6 99.7 %all-gather.8.cloned.1.call-start = ((), (), s32[]{:S(2)}) async-start(), calls=%async_computation.6 | async-start | bytes 1474560 | tf_op jit(solution)/shard_map/all_gather | solution.py:134
  10.3 137.8 %all-gather.14.cloned.1.call-start = ((), (), s32[]{:S(2)}) async-start(), calls=%async_computation.9 | async-start | bytes 1474560 | tf_op jit(solution)/shard_map/all_gather | solution.py:136
  10.9 216.6 %all-gather.16.cloned.1.call-start = ((), (), s32[]{:S(2)}) async-start(), calls=%async_computation.10 | async-start | bytes 5898240 | tf_op jit(solution)/shard_map/all_gather | solution.py:140
  11.5 305.5 %all-gather.18.cloned.1.call-start = ((), (), s32[]{:S(2)}) async-start(), calls=%async_computation.11 | async-start | bytes 5898240 | tf_op jit(solution)/shard_map/all_gather | solution.py:142
  12.1 578.4 %reduce-scatter.13.cloned.1.call-start = ((), (), s32[]{:S(2)}) async-start(), calls=%async_computation.15 | async-start | bytes 1474560 | tf_op jit(solution)/shard_map/reduce_scatter | solution.py:327
  38.1 71.2 %copy-start.30 = (f32[768]{0:T(1024)}, f32[768]{0:T(1024)S(1)}, u32[]{:S(2)}) copy-start(f32[768]{0:T(1024)S(1)} %convert_element_type.260) | copy-start | bytes 9220
  38.1 71.2 %copy-start.41 = (f32[768]{0:T(1024)}, f32[768]{0:T(1024)S(1)}, u32[]{:S(2)}) copy-start(f32[768]{0:T(1024)S(1)} %convert_element_type.261) | copy-start | bytes 9220
  40.0 108.1 %copy-start.1 = (bf16[1,1024,768]{1,2,0:T(8,128)(2,1)}, bf16[1,1024,768]{1,2,0:T(8,128)(2,1)S(1)}, u32[]{:S(2)}) copy-start(bf16[1,1024,768]{1,2,0:T(8,128)(2,1)S(1)} %copy.48) | copy-start | bytes 4718596
  40.3 69.0 %copy-start.32 = (f32[1024]{0:T(1024)}, f32[1024]{0:T(1024)S(1)}, u32[]{:S(2)}) copy-start(f32[1024]{0:T(1024)S(1)} %broadcast_multiply_fusion.5) | copy-start | bytes 12292
  40.8 68.5 %copy-start.34 = (f32[1024]{0:T(1024)}, f32[1024]{0:T(1024)S(1)}, u32[]{:S(2)}) copy-start(f32[1024]{0:T(1024)S(1)} %add_rsqrt_fusion.1) | copy-start | bytes 12292
  42.7 93.1 %copy-start.36 = (pred[1024]{0:T(1024)(128)(4,1)}, pred[1024]{0:T(1024)(128)(4,1)S(1)}, u32[]{:S(2)}) copy-start(pred[1024]{0:T(1024)(128)(4,1)S(1)} %iota_compare_fusion) | copy-start | bytes 3076
  42.8 184.8 %copy-start.43 = (f32[768]{0:T(1024)}, f32[768]{0:T(1024)S(1)}, u32[]{:S(2)}) copy-start(f32[768]{0:T(1024)S(1)} %convert_element_type.273) | copy-start | bytes 9220
  60.6 28.1 %copy-start.7 = (bf16[1024,768]{0,1:T(8,128)(2,1)}, bf16[1024,768]{0,1:T(8,128)(2,1)S(1)}, u32[]{:S(2)}) copy-start(bf16[1024,768]{0,1:T(8,128)(2,1)S(1)} %convolution_convert_fusion.3) | copy-start | bytes 4718596
  112.2 23.6 %copy-start.8 = (bf16[1024,768]{0,1:T(8,128)(2,1)}, bf16[1024,768]{0,1:T(8,128)(2,1)S(1)}, u32[]{:S(2)}) copy-start(bf16[1024,768]{0,1:T(8,128)(2,1)S(1)} %add_convert_fusion.4) | copy-start | bytes 4718596
  124.2 23.5 %copy-start.24 = (bf16[12,64,512]{2,1,0:T(8,128)(2,1)}, bf16[12,64,512]{2,1,0:T(8,128)(2,1)S(1)}, u32[]{:S(2)}) copy-start(bf16[12,64,512]{2,1,0:T(8,128)(2,1)S(1)} %fusion.67) | copy-start | bytes 2359300
  227.6 89.4 %copy-start.12 = (bf16[1,1024,768]{2,1,0:T(8,128)(2,1)S(1)}, bf16[1,1024,768]{2,1,0:T(8,128)(2,1)}, u32[]{:S(2)}) copy-start(bf16[1,1024,768]{2,1,0:T(8,128)(2,1)} %param.21) | copy-start | bytes 4718596
  356.7 233.8 %reduce-scatter.7.cloned.1.call-start = ((), (), s32[]{:S(2)}) async-start(), calls=%async_computation.12 | async-start | bytes 1474560 | tf_op jit(solution)/shard_map/reduce_scatter | solution.py:312
  469.1 121.4 %reduce-scatter.9.cloned.1.call-start = ((), (), s32[]{:S(2)}) async-start(), calls=%async_computation.13 | async-start | bytes 1474560 | tf_op jit(solution)/shard_map/reduce_scatter | solution.py:318
  487.7 102.8 %reduce-scatter.11.cloned.1.call-start = ((), (), s32[]{:S(2)}) async-start(), calls=%async_computation.14 | async-start | bytes 1474560 | tf_op jit(solution)/shard_map/reduce_scatter | solution.py:321
  513.7 130.4 %reduce-scatter.15.cloned.1.call-start = ((), (), s32[]{:S(2)}) async-start(), calls=%async_computation.16 | async-start | bytes 5898240 | tf_op jit(solution)/shard_map/reduce_scatter | solution.py:339
  523.9 208.6 %reduce-scatter.17.cloned.1.call-start = ((), (), s32[]{:S(2)}) async-start(), calls=%async_computation.17 | async-start | bytes 5898240 | tf_op jit(solution)/shard_map/reduce_scatter | solution.py:345
  535.1 342.8 %all-reduce.23.cloned.1.call-start = ((), (), s32[]{:S(2)}) async-start(), calls=%async_computation.18 | async-start | bytes 294912 | tf_op jit(solution)/shard_map/psum | solution.py:374
  (49 other events, 252.9 us)
Sparse Core Ops, SparseCore 0:
  10.5 33.1 all-gather.11
  45.3 30.0 all-gather.9
  77.0 29.5 all-gather.7
  108.0 29.5 all-gather.13
  139.0 88.5 all-gather.15
  229.0 87.9 all-gather.17
  356.8 27.6 reduce-scatter.12
  469.2 27.5 reduce-scatter.6
  499.2 27.8 reduce-scatter.8
  529.3 27.9 reduce-scatter.10
  559.6 84.5 reduce-scatter.14
  646.3 86.1 reduce-scatter.16
Sparse Core Ops, SparseCore 1:
  542.6 249.9 all-reduce.22
where the time goes:
time: 892 us; the launch traced here: 887 us
  waiting for transfers between devices  286 us (32%)
  matrix products  280 us (31%)
  blocking collectives  196 us (22%)
  other arithmetic  75.3 us (8%)
  local copies, waits for them, and re-layouts  27.4 us (3%)
  between operations  20.8 us (2%)
    psum x1, blocking collectives, body(): lax.psum((shard_grads[0], shard_grads[1], shard_grads[2], shard_grads[3],...  145 us
    reduce_scatter x1, waiting for transfers between devices, body(): lax.psum_scatter(local_grads[13].astype(jnp.bfloat16), 'fsdp', scatter_di...  88.4 us
    all_gather x1, waiting for transfers between devices, body(): lax.all_gather(shards[11], 'fsdp', axis=0, tiled=True)  74.3 us
    dot_general x6, matrix products, project(): jnp.einsum('csd,de->cse', rows, matrix, preferred_element_type=jnp.float32)  59.4 us
    reduce_scatter x1, waiting for transfers between devices, body(): lax.psum_scatter(local_grads[11].astype(jnp.bfloat16), 'fsdp', scatter_di...  53.6 us
    all_gather x1, waiting for transfers between devices, body(): lax.all_gather(shards[13], 'fsdp', axis=0, tiled=True)  51.2 us
    dot_general x2, matrix products, attend_backward(): jnp.einsum('cqhe,ckhe->chqk', grad_block, value_rows, preferred_element_t...  45.8 us
    convert_element_type x1, other arithmetic, attend_backward(): grad_scores = (shares * (grad_shares - inner)).astype(jnp.bfloat16)  41.7 us
  transfers between devices with their start and end apart: 13, of which 5 were waited for; matrix products, arithmetic and copies ran while one was open for 38% of the time, Pallas kernels for 0%

commit v1 on v0

--- a/solution.py
+++ b/solution.py
@@ -3,6 +3,8 @@
 import jax
 import jax.numpy as jnp
 from jax import lax
+from jax.experimental import pallas as pl
+from jax.experimental.pallas import tpu as pltpu
 from jax.sharding import PartitionSpec as P
 
 HEADS = 12
@@ -45,45 +47,81 @@
     return jnp.sum(values.astype(jnp.float32), axis=(0, 1))
 
 
-def masked_scores(query_block, key_rows, key_live, factor):
-    scores = (
-        jnp.einsum("cqhe,ckhe->chqk", query_block, key_rows, preferred_element_type=jnp.float32)
-        * factor
-    )
-    return jnp.where(key_live[:, None, None, :], scores, NEGATIVE)
-
-
-def attend_forward(query_block, key_rows, value_rows, key_live, factor):
-    scores = masked_scores(query_block, key_rows, key_live, factor)
-    largest = jnp.max(scores, axis=-1, keepdims=True)
-    raised = jnp.exp(scores - largest)
-    summed = jnp.sum(raised, axis=-1, keepdims=True)
-    shares = (raised / summed).astype(jnp.bfloat16)
-    blended = jnp.einsum("chqk,ckhe->cqhe", shares, value_rows, preferred_element_type=jnp.float32)
-    return (blended, largest + jnp.log(summed))
-
-
-def attend_backward(query_block, grad_block, key_rows, value_rows, key_live, log_total, factor):
-    scores = masked_scores(query_block, key_rows, key_live, factor)
-    shares = jnp.exp(scores - log_total)
-    grad_values = jnp.einsum(
-        "chqk,cqhe->ckhe",
-        shares.astype(jnp.bfloat16),
-        grad_block,
-        preferred_element_type=jnp.float32,
-    )
-    grad_shares = jnp.einsum(
-        "cqhe,ckhe->chqk", grad_block, value_rows, preferred_element_type=jnp.float32
-    )
-    inner = jnp.sum(shares * grad_shares, axis=-1, keepdims=True)
-    grad_scores = (shares * (grad_shares - inner)).astype(jnp.bfloat16)
-    grad_queries = factor * jnp.einsum(
-        "chqk,ckhe->cqhe", grad_scores, key_rows, preferred_element_type=jnp.float32
-    )
-    grad_keys = factor * jnp.einsum(
-        "chqk,cqhe->ckhe", grad_scores, query_block, preferred_element_type=jnp.float32
-    )
-    return (grad_queries, grad_keys, grad_values)
+def fwd_kernel(qb, len_ref, q_ref, k_ref, v_ref, o_ref, e_ref, r_ref):
+    S=k_ref.shape[0]
+    lane = lax.broadcasted_iota(jnp.int32,(S,128),1)
+    kpos = lax.broadcasted_iota(jnp.int32,(1,S),1)
+    bias = jnp.where(kpos < len_ref[0], 0.0, -1e30).astype(jnp.float32)
+    k = k_ref[...]
+    v = v_ref[...]
+    first = lane < 64
+    k0 = jnp.where(first, k, jnp.zeros_like(k)); k1 = jnp.where(first, jnp.zeros_like(k), k)
+    fq = lax.broadcasted_iota(jnp.int32,(qb,128),1) < 64
+    for b in range(S//qb):
+        rows = pl.ds(b*qb, qb)
+        q = q_ref[rows,:]
+        outs=[]; rs=[]
+        for h,kh in ((0,k0),(1,k1)):
+            s = lax.dot_general(q, kh, (((1,),(1,)),((),())), preferred_element_type=jnp.float32) + bias
+            m = jnp.max(s, axis=1, keepdims=True)
+            e = jnp.exp(s-m)
+            l = jnp.sum(e, axis=1, keepdims=True)
+            eb = e.astype(jnp.bfloat16)
+            e_ref[h, rows, :] = eb
+            o = jnp.dot(eb, v, preferred_element_type=jnp.float32)
+            outs.append(o); rs.append(1.0/l)
+        r = jnp.where(fq, rs[0], rs[1])
+        r_ref[rows,:] = r
+        o_ref[rows,:] = (jnp.where(fq, outs[0], outs[1])*r).astype(jnp.bfloat16)
+def attn_fwd(length, q, k, v, qb=256):
+    S,D=q.shape; pairs=D//128
+    blk=pl.BlockSpec((S,128), lambda p: (0,p))
+    return pl.pallas_call(partial(fwd_kernel,qb), grid=(pairs,),
+        in_specs=[pl.BlockSpec(memory_space=pltpu.SMEM), blk, blk, blk],
+        out_specs=[blk, pl.BlockSpec((2,S,S), lambda p:(p,0,0)), blk],
+        out_shape=[jax.ShapeDtypeStruct((S,D),jnp.bfloat16), jax.ShapeDtypeStruct((2*pairs,S,S),jnp.bfloat16), jax.ShapeDtypeStruct((S,D),jnp.float32)],
+        compiler_params=pltpu.CompilerParams(vmem_limit_bytes=56<<20), name="attn_fwd")(length,q,k,v)
+
+def bwd_kernel(qb, q_ref, k_ref, v_ref, do_ref, o_ref, r_ref, e_ref, dq_ref, dk_ref, dv_ref, kt_acc, vt_acc):
+    S=k_ref.shape[0]
+    lane = lax.broadcasted_iota(jnp.int32,(S,128),1); first = lane<64
+    fq = lax.broadcasted_iota(jnp.int32,(qb,128),1) < 64
+    k=k_ref[...]; v=v_ref[...]
+    z=jnp.zeros_like(k)
+    v0=jnp.where(first,v,z); v1=jnp.where(first,z,v)
+    for b in range(S//qb):
+        rows=pl.ds(b*qb,qb)
+        do = do_ref[rows,:].astype(jnp.float32)*r_ref[rows,:]
+        dob = do.astype(jnp.bfloat16)
+        prod = dob.astype(jnp.float32)*o_ref[rows,:].astype(jnp.float32)
+        dall = jnp.sum(prod,axis=1,keepdims=True)
+        d0 = jnp.sum(jnp.where(fq,prod,0.0),axis=1,keepdims=True); d1=dall-d0
+        dot_ = dob.T
+        qt = q_ref[rows,:].T
+        dqs=[]
+        for h,vh,d in ((0,v0,d0),(1,v1,d1)):
+            e = e_ref[h,rows,:]
+            dp = lax.dot_general(dob, vh, (((1,),(1,)),((),())), preferred_element_type=jnp.float32)
+            ds = (e.astype(jnp.float32)*(dp-d)).astype(jnp.bfloat16)
+            dqs.append(jnp.dot(ds,k,preferred_element_type=jnp.float32))
+            hr = slice(h*64,h*64+64)
+            dv_t = jnp.dot(dot_[hr], e, preferred_element_type=jnp.float32)
+            dk_t = jnp.dot(qt[hr], ds, preferred_element_type=jnp.float32)
+            if b==0:
+                vt_acc[hr,:]=dv_t; kt_acc[hr,:]=dk_t
+            else:
+                vt_acc[hr,:]+=dv_t; kt_acc[hr,:]+=dk_t
+        dq_ref[rows,:] = (jnp.where(fq,dqs[0],dqs[1])*0.125).astype(jnp.bfloat16)
+    dk_ref[...] = kt_acc[...].astype(jnp.bfloat16).T
+    dv_ref[...] = vt_acc[...].astype(jnp.bfloat16).T
+def attn_bwd(q,k,v,do,o,r,e,qb=256):
+    S,D=q.shape; pairs=D//128
+    blk=pl.BlockSpec((S,128), lambda p: (0,p))
+    return pl.pallas_call(partial(bwd_kernel,qb), grid=(pairs,),
+        in_specs=[blk]*6+[pl.BlockSpec((2,S,S), lambda p:(p,0,0))],
+        out_specs=[blk]*3, out_shape=[jax.ShapeDtypeStruct((S,D),jnp.bfloat16)]*3,
+        scratch_shapes=[pltpu.VMEM((128,S),jnp.float32)]*2,
+        compiler_params=pltpu.CompilerParams(vmem_limit_bytes=56<<20), name="attn_bwd")(q,k,v,do,o,r,e)
 
 
 def body(
@@ -184,15 +222,11 @@
         .astype(jnp.bfloat16)
         .reshape(head_shape)
     )
-    blended_parts = []
-    log_parts = []
-    for begin in range(0, seq_length, block_rows):
-        query_block = query_rows[:, begin : begin + block_rows]
-        blended, log_total = attend_forward(query_block, key_rows, value_rows, key_live, factor)
-        blended_parts.append(blended)
-        log_parts.append(log_total)
-    attn_out = jnp.concatenate(blended_parts, axis=1).reshape(cell_count, seq_length, model_width)
-    attn_out = attn_out.astype(jnp.bfloat16)
+    query_flat = query_rows.reshape(seq_length, model_width) * jnp.asarray(factor, jnp.bfloat16)
+    key_flat = key_rows.reshape(seq_length, model_width)
+    value_flat = value_rows.reshape(seq_length, model_width)
+    attn_flat, raised, inverse_sum = attn_fwd(cell_lens.astype(jnp.int32), query_flat, key_flat, value_flat, 512)
+    attn_out = attn_flat[None]
     residual = inputs + project(attn_out, out_w) + out_b.astype(jnp.float32)
     normed_two, inverse_two = normalize(residual)
     ffn_in = (normed_two * gain_two.astype(jnp.float32) + shift_two.astype(jnp.float32)).astype(
@@ -253,22 +287,13 @@
     grad_out_w = outer_sum(attn_out, grad_branch)
     grad_out_b = row_total(grad_branch)
     grad_mixed = project_back(grad_branch, out_wb).astype(jnp.bfloat16).reshape(head_shape)
-    grad_keys = jnp.zeros(head_shape, jnp.float32)
-    grad_values = jnp.zeros(head_shape, jnp.float32)
-    query_parts = []
-    for number, begin in enumerate(range(0, seq_length, block_rows)):
-        query_block = query_rows[:, begin : begin + block_rows]
-        grad_block = grad_mixed[:, begin : begin + block_rows]
-        part_queries, part_keys, part_values = attend_backward(
-            query_block, grad_block, key_rows, value_rows, key_live, log_parts[number], factor
+    grad_query_rows, grad_key_rows, grad_value_rows = (
+        part[None]
+        for part in attn_bwd(
+            query_flat, key_flat, value_flat, grad_mixed.reshape(seq_length, model_width),
+            attn_flat, inverse_sum, raised, 512,
         )
-        query_parts.append(part_queries)
-        grad_keys = grad_keys + part_keys
-        grad_values = grad_values + part_values
-    flat_shape = (cell_count, seq_length, model_width)
-    grad_query_rows = jnp.concatenate(query_parts, axis=1).reshape(flat_shape).astype(jnp.bfloat16)
-    grad_key_rows = grad_keys.reshape(flat_shape).astype(jnp.bfloat16)
-    grad_value_rows = grad_values.reshape(flat_shape).astype(jnp.bfloat16)
+    )
     grad_query_w = outer_sum(attn_in, grad_query_rows)
     grad_query_b = row_total(grad_query_rows)
     grad_key_w = outer_sum(attn_in, grad_key_rows)

time: 892 us -> 813 us (0.911)
  matrix products: 280 us -> 133 us
  waiting for transfers between devices: 286 us -> 361 us
  other arithmetic: 75.3 us -> 20.8 us
  Pallas kernels: 0 us -> 54 us
    dot_general x12 -> x0, matrix products: 153 us -> none  [the longest x2 45.8 us: attend_backward(): jnp.einsum('cqhe,ckhe->chqk', grad_block, value_rows, preferred_element_t...]
    pallas_call x0 -> x2, Pallas kernels: none -> 54 us  [the longest x1 27.8 us: attn_bwd(): pl.pallas_call(partial(bwd_kernel, qb), grid=(pairs,), in_specs=[blk] * 6...]
    convert_element_type x1 -> x0, other arithmetic: 41.7 us -> none  [attend_backward(): grad_scores = (shares * (grad_shares - inner)).astype(jnp.bfloat16)]
    reduce_scatter x1, waiting for transfers between devices: 53.6 us -> 86.9 us  [body(): lax.psum_scatter(local_grads[11].astype(jnp.bfloat16), 'fsdp', scatter_di...]
    all_gather x1, waiting for transfers between devices: 0.01 us -> 14.3 us  [body(): lax.all_gather(shards[5], 'fsdp', axis=0, tiled=True)]
    all_gather x1, waiting for transfers between devices: 14.8 us -> 27.1 us  [body(): lax.all_gather(shards[2], 'fsdp', axis=0, tiled=True)]
    reduce_sum x1 -> x0, other arithmetic: 11.5 us -> none  [attend_forward(): summed = jnp.sum(raised, axis=-1, keepdims=True)]
    all_gather x1, waiting for transfers between devices: 74.3 us -> 84.5 us  [body(): lax.all_gather(shards[11], 'fsdp', axis=0, tiled=True)]
  transfers between devices with their start and end apart: 13 -> 13, of which waited for: 5 -> 8; matrix products, arithmetic and copies ran while one was open for 38% -> 17% of each run, Pallas kernels for 0% -> 7%
where the time goes in v1:
time: 813 us; the launch traced here: 809 us
  waiting for transfers between devices  361 us (44%)
  blocking collectives  196 us (24%)
  matrix products  133 us (16%)
  Pallas kernels  54 us (7%)
  local copies, waits for them, and re-layouts  23.5 us (3%)
  other arithmetic  20.8 us (3%)
  between operations  20.4 us (3%)
    psum x1, blocking collectives, body(): lax.psum((shard_grads[0], shard_grads[1], shard_grads[2], shard_grads[3],...  145 us
    reduce_scatter x1, waiting for transfers between devices, body(): lax.psum_scatter(local_grads[13].astype(jnp.bfloat16), 'fsdp', scatter_di...  88.3 us
    reduce_scatter x1, waiting for transfers between devices, body(): lax.psum_scatter(local_grads[11].astype(jnp.bfloat16), 'fsdp', scatter_di...  86.9 us
    all_gather x1, waiting for transfers between devices, body(): lax.all_gather(shards[11], 'fsdp', axis=0, tiled=True)  84.5 us
    dot_general x6, matrix products, project(): jnp.einsum('csd,de->cse', rows, matrix, preferred_element_type=jnp.float32)  63.2 us
    all_gather x1, waiting for transfers between devices, body(): lax.all_gather(shards[13], 'fsdp', axis=0, tiled=True)  51.4 us
    unnamed x2, blocking collectives  38.1 us
    dot_general x6, matrix products, project_back(): jnp.einsum('cse,de->csd', grads, matrix, preferred_element_type=jnp.float32)  37.1 us
  transfers between devices with their start and end apart: 13, of which 8 were waited for; matrix products, arithmetic and copies ran while one was open for 17% of the time, Pallas kernels for 7%

profile of v1, /device:TPU:0, one launch (start us, length us, event | category | flops | bytes accessed | tf_op | source)
XLA Modules:
  0.0 808.9 jit_solution(382499215170420566)
XLA Ops:
  17.0 21.2 %all-reduce.19 = (bf16[768]{0:T(1024)(128)(2,1)S(1)}, bf16[768]{0:T(1024)(128)(2,1)S(1)}, bf16[768]{0:T(1024)(128)(2,1)S(1)}, bf16[768]{0:T(1024)(128)(2,1)S(1)}...) all-reduce(bf16[768]{0:T(1024)(128)(2,1)S(1)} %dynamic-update-slice, ...), channel_id=1, replica_groups=mesh['dp'=8,'fsdp'=4] {'fsdp'}, use_global_device_ids=true, to_apply=%add.2 | all-reduce | flops 5376 | bytes 21504
  40.9 13.2 %all-gather = bf16[4,1,768]{2,1,0:T(2,128)(2,1)S(1)} all-gather(bf16[1,1,768]{2,1,0:T(2,128)(2,1)S(1)} %reshape.378), channel_id=1, replica_groups=mesh['dp'=8,'fsdp'=4] {'fsdp'}, dimensions={0}, use_global_device_ids=true | all-gather | bytes 7680 | tf_op jit(solution)/shard_map/all_gather | solution.py:179
  61.1 14.3 %all-gather.12.cloned.1.call-done = bf16[768,768]{1,0:T(8,128)(2,1)} async-done(((bf16[192,768]{1,0:T(8,128)(2,1)}), bf16[768,768]{1,0:T(8,128)(2,1)}) %all-gather.12.cloned.1.call-update) | async-done | bytes 1179664 | tf_op jit(solution)/shard_map/all_gather | solution.py:172
  75.4 4.1 add_convert_fusion.2.v_ref
  79.5 27.1 %all-gather.8.cloned.1.call-done = bf16[768,768]{1,0:T(8,128)(2,1)} async-done(((bf16[192,768]{1,0:T(8,128)(2,1)}), bf16[768,768]{1,0:T(8,128)(2,1)}) %all-gather.8.cloned.1.call-update) | async-done | bytes 1179664 | tf_op jit(solution)/shard_map/all_gather | solution.py:169
  106.6 4.1 fusion.38.q_ref
  110.7 26.2 %attn_fwd.1 = (bf16[1024,768]{1,0:T(8,128)(2,1)}, bf16[12,1024,1024]{2,1,0:T(8,128)(2,1)}, f32[1024,768]{1,0:T(8,128)}) custom-call(s32[1]{0:T(128)} %dynamic-slice.5.len_ref, bf16[1024,768]{1,0:T(8,128)(2,1)} %fusion.38.q_ref, bf16[1024,768]{1,0:T(8,128)(2,1)} %convolution_convert_fusion.3.k_ref, bf16[1024,768]{1,0:T(8,128)(2,1)} %add_convert_fusion.2.v_ref), custom_call_target="tpu_custom_call" | custom-call | tf_op jit(solution)/shard_map/attn_fwd/pallas_call | solution.py:79
  143.1 84.5 %all-gather.16.cloned.1.call-done = bf16[768,3072]{1,0:T(8,128)(2,1)} async-done(((bf16[192,3072]{1,0:T(8,128)(2,1)}), bf16[768,3072]{1,0:T(8,128)(2,1)}) %all-gather.16.cloned.1.call-update) | async-done | bytes 4718608 | tf_op jit(solution)/shard_map/all_gather | solution.py:178
  227.6 37.9 %multiply_convert_fusion = (bf16[1024,3072]{1,0:T(8,128)(2,1)}, f32[1024,3072]{1,0:T(8,128)}, f32[1024,3072]{1,0:T(8,128)}) fusion(f32[3072]{0:T(1024)S(1)} %bitcast.89, bf16[768,3072]{1,0:T(8,128)(2,1)} %all-gather.16.cloned.1.call-done, f32[1,1024,768]{1,2,0:T(8,128)} %copy-done.3, f32[768]{0:T(1024)S(1)} %convert_element_type.176, ...), kind=kOutput, calls=%fused_computation.4 | convolution fusion | flops 5043388416 | bytes 39348224 | tf_op jit(solution)/shard_map/csd,de->cse/dot_general | solution.py:35
  265.5 51.4 %all-gather.18.cloned.1.call-done = bf16[3072,768]{1,0:T(8,128)(2,1)} async-done(((bf16[768,768]{1,0:T(8,128)(2,1)}), bf16[3072,768]{1,0:T(8,128)(2,1)}) %all-gather.18.cloned.1.call-update) | async-done | bytes 4718608 | tf_op jit(solution)/shard_map/all_gather | solution.py:180
  316.9 16.9 %fusion.59 = (bf16[3072]{0:T(1024)(128)(2,1)S(1)}, bf16[1024,3072]{1,0:T(8,128)(2,1)}) fusion(f32[1024,3072]{1,0:T(8,128)} %get-tuple-element.129, bf16[3072,768]{1,0:T(8,128)(2,1)} %all-gather.18.cloned.1.call-done, bf16[1,1024,768]{2,1,0:T(8,128)(2,1)S(1)} %copy-done.8, f32[1024,3072]{1,0:T(8,128)} %get-tuple-element.134, f32[3072]{0:T(1024)S(1)} %bitcast.90), kind=kOutput, calls=%fused_computation.100 | convolution fusion | flops 4882166784 | bytes 37767168 | tf_op jit(solution)/shard_map/cse,de->csd/dot_general | solution.py:39
  333.8 8.9 %fusion.58 = (bf16[768]{0:T(1024)(128)(2,1)S(1)}, f32[1024,768]{1,0:T(8,128)}) fusion(bf16[1024,3072]{1,0:T(8,128)(2,1)} %get-tuple-element.139, bf16[768,3072]{1,0:T(8,128)(2,1)S(1)} %copy-done.23), kind=kOutput, calls=%fused_computation.99 | convolution fusion | flops 4832623616 | bytes 14157312 | tf_op jit(solution)/shard_map/cse,de->csd/dot_general | solution.py:39
  354.0 4.6 convolution_convert_fusion.2.do_ref
  358.6 27.8 %attn_bwd.1 = (bf16[1024,768]{1,0:T(8,128)(2,1)}, bf16[1024,768]{1,0:T(8,128)(2,1)}, bf16[1024,768]{1,0:T(8,128)(2,1)}) custom-call(bf16[1024,768]{1,0:T(8,128)(2,1)} %fusion.38.q_ref, bf16[1024,768]{1,0:T(8,128)(2,1)} %convolution_convert_fusion.3.k_ref, bf16[1024,768]{1,0:T(8,128)(2,1)} %add_convert_fusion.2.v_ref, ...), custom_call_target="tpu_custom_call" | custom-call | tf_op jit(solution)/shard_map/attn_bwd/pallas_call | solution.py:120
  390.5 4.1 convolution_convert_fusion.5
  397.5 9.9 %convolution_convert_fusion.1 = bf16[768,3072]{1,0:T(8,128)(2,1)} fusion(bf16[1024,3072]{1,0:T(8,128)(2,1)} %get-tuple-element.139, f32[1,1024,768]{1,2,0:T(8,128)} %copy-done.3, f32[768]{0:T(1024)S(1)} %convert_element_type.176, f32[768]{0:T(1024)S(1)} %convert_element_type.175, f32[1024]{0:T(1024)S(1)} %add_rsqrt_fusion, ...), kind=kOutput, calls=%fused_computation.19 | convolution fusion | flops 4838129664 | bytes 14170112 | tf_op jit(solution)/shard_map/csd,cse->de/dot_general | solution.py:43
  407.4 9.4 %convolution_convert_fusion = bf16[3072,768]{1,0:T(8,128)(2,1)} fusion(bf16[1024,3072]{1,0:T(8,128)(2,1)} %get-tuple-element.128, bf16[1,1024,768]{2,1,0:T(8,128)(2,1)} %param.21), kind=kOutput, calls=%fused_computation.18 | convolution fusion | flops 4834197504 | bytes 12582912 | tf_op jit(solution)/shard_map/csd,cse->de/dot_general | solution.py:43
  417.6 6.7 scatter_custom_fusion
  438.5 5.0 fusion.18
  446.3 16.9 %all-reduce.18 = (bf16[768]{0:T(1024)(128)(2,1)S(1)}, bf16[768]{0:T(1024)(128)(2,1)S(1)}, bf16[768]{0:T(1024)(128)(2,1)S(1)}, bf16[768]{0:T(1024)(128)(2,1)S(1)}...) all-reduce(bf16[768]{0:T(1024)(128)(2,1)S(1)} %dynamic-update-slice, ...), channel_id=1, replica_groups=mesh['dp'=8,'fsdp'=4] {'fsdp'}, use_global_device_ids=true, to_apply=%add.7 | all-reduce | flops 9984 | bytes 39936
  463.2 9.6 %fusion.27 = bf16[1,1024,768]{1,2,0:T(8,128)(2,1)} fusion(f32[1,1024,768]{1,2,0:T(8,128)S(1)} %copy-done.5, bf16[1024,3072]{1,0:T(8,128)(2,1)} %get-tuple-element.128, bf16[3072,768]{1,0:T(8,128)(2,1)} %all-gather.18.cloned.1.call-done, f32[768]{0:T(1024)S(1)} %convert_element_type.180), kind=kOutput, calls=%fused_computation.48 | convolution fusion | flops 4834197504 | bytes 15731712 | tf_op jit(solution)/shard_map/csd,de->cse/dot_general | solution.py:35
  479.5 86.9 %reduce-scatter.15.cloned.1.call-done = bf16[192,3072]{1,0:T(8,128)(2,1)} async-done(((bf16[768,3072]{1,0:T(8,128)(2,1)}), bf16[192,3072]{1,0:T(8,128)(2,1)}) %reduce-scatter.15.cloned.1.call-update) | async-done | bytes 1179664 | tf_op jit(solution)/shard_map/reduce_scatter | solution.py:364
  566.4 88.3 %reduce-scatter.17.cloned.1.call-done = bf16[768,768]{1,0:T(8,128)(2,1)} async-done(((bf16[3072,768]{1,0:T(8,128)(2,1)}), bf16[768,768]{1,0:T(8,128)(2,1)}) %reduce-scatter.17.cloned.1.call-update) | async-done | bytes 1179664 | tf_op jit(solution)/shard_map/reduce_scatter | solution.py:370
  654.7 144.9 %all-reduce.24 = (f32[192]{0:T(256)}, f32[192]{0:T(256)}, f32[192,768]{1,0:T(8,128)}, f32[192]{0:T(256)}, f32[192,768]{1,0:T(8,128)}, /*index=5*/f32[192,768]{1,...) all-reduce(f32[192]{0:T(256)S(1)} %get-tuple-element.147, ...), channel_id=1, replica_groups=mesh['dp'=8,'fsdp'=4] {'dp'}, use_global_device_ids=true, to_apply=%region_10.0 | all-reduce | flops 1771776 | bytes 10635264 | tf_op jit(solution)/shard_map/psum | solution.py:377
  (171 shorter events, 64.6 us)
Async XLA Ops:
  8.1 48.9 %all-gather.10.cloned.1.call-start = ((), (), s32[]{:S(2)}) async-start(), calls=%async_computation.7 | async-start | bytes 1474560 | tf_op jit(solution)/shard_map/all_gather | solution.py:171
  8.9 66.6 %all-gather.12.cloned.1.call-start = ((), (), s32[]{:S(2)}) async-start(), calls=%async_computation.8 | async-start | bytes 1474560 | tf_op jit(solution)/shard_map/all_gather | solution.py:172
  9.6 97.0 %all-gather.8.cloned.1.call-start = ((), (), s32[]{:S(2)}) async-start(), calls=%async_computation.6 | async-start | bytes 1474560 | tf_op jit(solution)/shard_map/all_gather | solution.py:169
  10.3 127.3 %all-gather.14.cloned.1.call-start = ((), (), s32[]{:S(2)}) async-start(), calls=%async_computation.9 | async-start | bytes 1474560 | tf_op jit(solution)/shard_map/all_gather | solution.py:174
  10.9 216.7 %all-gather.16.cloned.1.call-start = ((), (), s32[]{:S(2)}) async-start(), calls=%async_computation.10 | async-start | bytes 5898240 | tf_op jit(solution)/shard_map/all_gather | solution.py:178
  11.5 305.4 %all-gather.18.cloned.1.call-start = ((), (), s32[]{:S(2)}) async-start(), calls=%async_computation.11 | async-start | bytes 5898240 | tf_op jit(solution)/shard_map/all_gather | solution.py:180
  12.1 463.7 %reduce-scatter.13.cloned.1.call-start = ((), (), s32[]{:S(2)}) async-start(), calls=%async_computation.15 | async-start | bytes 1474560 | tf_op jit(solution)/shard_map/reduce_scatter | solution.py:352
  38.1 68.5 %copy-start.17 = (f32[768]{0:T(1024)}, f32[768]{0:T(1024)S(1)}, u32[]{:S(2)}) copy-start(f32[768]{0:T(1024)S(1)} %convert_element_type.166) | copy-start | bytes 9220
  38.1 68.5 %copy-start.19 = (f32[768]{0:T(1024)}, f32[768]{0:T(1024)S(1)}, u32[]{:S(2)}) copy-start(f32[768]{0:T(1024)S(1)} %convert_element_type.167) | copy-start | bytes 9220
  40.0 97.6 %copy-start = (bf16[1,1024,768]{1,2,0:T(8,128)(2,1)}, bf16[1,1024,768]{1,2,0:T(8,128)(2,1)S(1)}, u32[]{:S(2)}) copy-start(bf16[1,1024,768]{1,2,0:T(8,128)(2,1)S(1)} %copy.48) | copy-start | bytes 4718596
  40.3 66.3 %copy-start.13 = (f32[1024]{0:T(1024)}, f32[1024]{0:T(1024)S(1)}, u32[]{:S(2)}) copy-start(f32[1024]{0:T(1024)S(1)} %broadcast_multiply_fusion.5) | copy-start | bytes 12292
  40.8 65.8 %copy-start.15 = (f32[1024]{0:T(1024)}, f32[1024]{0:T(1024)S(1)}, u32[]{:S(2)}) copy-start(f32[1024]{0:T(1024)S(1)} %add_rsqrt_fusion.1) | copy-start | bytes 12292
  354.0 121.8 %reduce-scatter.7.cloned.1.call-start = ((), (), s32[]{:S(2)}) async-start(), calls=%async_computation.12 | async-start | bytes 1474560 | tf_op jit(solution)/shard_map/reduce_scatter | solution.py:337
  358.6 27.8 %copy-start.1 = (bf16[1,1024,768]{1,2,0:T(8,128)(2,1)S(1)}, bf16[1,1024,768]{1,2,0:T(8,128)(2,1)}, u32[]{:S(2)}) copy-start(bf16[1,1024,768]{1,2,0:T(8,128)(2,1)} %copy-done) | copy-start | bytes 4718596
  358.6 27.8 %copy-start.14 = (f32[1024]{0:T(1024)S(1)}, f32[1024]{0:T(1024)}, u32[]{:S(2)}) copy-start(f32[1024]{0:T(1024)} %copy-done.13) | copy-start | bytes 12292
  358.6 27.8 %copy-start.16 = (f32[1024]{0:T(1024)S(1)}, f32[1024]{0:T(1024)}, u32[]{:S(2)}) copy-start(f32[1024]{0:T(1024)} %copy-done.15) | copy-start | bytes 12292
  358.6 27.8 %copy-start.18 = (f32[768]{0:T(1024)S(1)}, f32[768]{0:T(1024)}, u32[]{:S(2)}) copy-start(f32[768]{0:T(1024)} %copy-done.17) | copy-start | bytes 9220
  358.6 27.8 %copy-start.20 = (f32[768]{0:T(1024)S(1)}, f32[768]{0:T(1024)}, u32[]{:S(2)}) copy-start(f32[768]{0:T(1024)} %copy-done.19) | copy-start | bytes 9220
  390.5 85.3 %reduce-scatter.9.cloned.1.call-start = ((), (), s32[]{:S(2)}) async-start(), calls=%async_computation.13 | async-start | bytes 1474560 | tf_op jit(solution)/shard_map/reduce_scatter | solution.py:343
  394.7 84.8 %reduce-scatter.11.cloned.1.call-start = ((), (), s32[]{:S(2)}) async-start(), calls=%async_computation.14 | async-start | bytes 1474560 | tf_op jit(solution)/shard_map/reduce_scatter | solution.py:346
  397.4 169.0 %reduce-scatter.15.cloned.1.call-start = ((), (), s32[]{:S(2)}) async-start(), calls=%async_computation.16 | async-start | bytes 5898240 | tf_op jit(solution)/shard_map/reduce_scatter | solution.py:364
  407.4 247.3 %reduce-scatter.17.cloned.1.call-start = ((), (), s32[]{:S(2)}) async-start(), calls=%async_computation.17 | async-start | bytes 5898240 | tf_op jit(solution)/shard_map/reduce_scatter | solution.py:370
  416.9 382.8 %all-reduce.23.cloned.1.call-start = ((), (), s32[]{:S(2)}) async-start(), calls=%async_computation.18 | async-start | bytes 294912 | tf_op jit(solution)/shard_map/psum | solution.py:399
  443.6 19.7 %copy-start.5 = (f32[1,1024,768]{1,2,0:T(8,128)S(1)}, f32[1,1024,768]{1,2,0:T(8,128)}, u32[]{:S(2)}) copy-start(f32[1,1024,768]{1,2,0:T(8,128)} %copy-done.3) | copy-start | bytes 9437188
  (25 other events, 154.5 us)
Sparse Core Ops, SparseCore 0:
  10.5 33.1 all-gather.9
  45.3 30.0 all-gather.11
  77.0 29.5 all-gather.7
  108.0 29.5 all-gather.13
  139.0 88.5 all-gather.15
  229.0 87.8 all-gather.17
  354.1 27.5 reduce-scatter.12
  390.6 27.8 reduce-scatter.6
  420.8 28.1 reduce-scatter.8
  451.2 28.2 reduce-scatter.10
  481.8 84.5 reduce-scatter.14
  568.6 86.0 reduce-scatter.16
Sparse Core Ops, SparseCore 1:
  424.4 262.0 all-reduce.22
